TPU v7x, 256 devices: a whole 4x4x8 slice. The times are simulated.
256 devices in a mesh: energy: 32 (over y, x, core), orb: 8 (over z).
Axes of the slice: x: 4, y: 4, z: 8, core: 2. Of those that a mesh axis runs over, the one named last changes fastest.
Arguments:
- green: float32 [32, 2, 2048, 2048], P('energy', None, 'orb'), may hold values from -0.75 to 0.75
- sigma: float32 [32, 16, 2, 128, 128], P('energy', 'orb'), may hold values from -0.375 to 0.375
- neighbours: int32 [256, 16], P('orb'), may hold values from 0 to 255, as said below
- phonon_shift: int32 [6], replicated, may hold values from 1 to 16
- phonon_weight: float32 [2, 6], replicated, may hold values from 0.1 to 0.6
- dham: float32 [4096, 3, 8, 8], P('orb'), may hold values from -2 to 2
Outputs:
- scattering: float32 [32, 4096, 128], P('energy', 'orb')
Inputs may be any that keep to these rules, and one draw needn't show every extreme that they name: neighbours[a, k] is an atom other than a within 8 atoms of a; every atom has a neighbour exactly 8 atoms away.
All inputs are finite; a program needn't handle non-finite values.
Results may differ from a plain program's by a relative error of at most 0.0003.
Values sent between devices are 32-bit elements; how exact they have to be, the bound alone decides.
A program may use at most 128 MiB of HBM per device.

v0:
```python
import functools

import jax
import jax.numpy as jnp
from jax import lax
from jax.experimental import pallas as pl
from jax.experimental.pallas import tpu as pltpu
from jax.sharding import PartitionSpec as P

W = 8
BS = 128
HALO = 32
LEVELS = 8
MESH = pl.DeviceIdType.MESH
HIGHEST = lax.Precision.HIGHEST
F32 = jnp.float32
BF16 = jnp.bfloat16


def split(x):
    high = x.astype(BF16)
    return high, (x - high.astype(F32)).astype(BF16)


def dot(a, b):
    return jnp.dot(a, b, preferred_element_type=F32)


def dot_nt(a, b):
    return lax.dot_general(a, b, (((1,), (1,)), ((), ())), preferred_element_type=F32)


def iota(shape, dim):
    return lax.broadcasted_iota(jnp.int32, shape, dim)


def main_kernel(
    ne, green, sigma, slab, nbt, shift, weight, out,
    ext, sig, acc, bx, xin, rcv, smeared, half, done, slab_v, nbt_v, zed, dlane, bd, kmat,
    loc_sem, sig_send, sig_recv, halo_send, halo_recv, x_send, x_recv,
    a_send, a_recv, b_send, b_recv,
):
    en = lax.axis_index("energy")
    me = lax.axis_index("orb")
    up = lax.rem(me + 1, LEVELS)
    down = lax.rem(me + LEVELS - 1, LEVELS)
    rows = green.shape[1]
    half_rows = rows // 2 + HALO

    barrier = pltpu.get_barrier_semaphore()
    for z in (up, down):
        pl.semaphore_signal(barrier, inc=1, device_id=(en, z), device_id_type=MESH)

    def greet(d, carry):
        pl.semaphore_signal(
            barrier, inc=1, device_id=(lax.rem(en + d, ne), me), device_id_type=MESH
        )
        return carry

    lax.fori_loop(1, ne, greet, 0)

    own_green = pltpu.make_async_copy(green, ext.at[:, pl.ds(HALO, rows), :], loc_sem.at[0])
    own_sigma = pltpu.make_async_copy(sigma, sig.at[pl.ds(2 * me, 2)], loc_sem.at[1])
    own_slab = pltpu.make_async_copy(slab, slab_v, loc_sem.at[2])
    own_nbt = pltpu.make_async_copy(nbt, nbt_v, loc_sem.at[3])
    own_slab.start()
    own_nbt.start()
    own_sigma.start()
    own_green.start()
    pl.semaphore_wait(barrier, ne + 1)

    def at_up(dev, t):
        return 2 * lax.rem(dev - t + 2 * LEVELS, LEVELS)

    def at_down(dev, t):
        return 2 * lax.rem(dev + t, LEVELS) + 1

    def sig_up(t, src=None):
        m = at_up(up, t)
        return pltpu.make_async_remote_copy(
            src_ref=sig.at[m] if src is None else src, dst_ref=sig.at[m],
            send_sem=sig_send.at[0, t], recv_sem=sig_recv.at[0, t],
            device_id=(en, up), device_id_type=MESH,
        )

    def sig_down(t, src=None):
        m = at_down(down, t)
        return pltpu.make_async_remote_copy(
            src_ref=sig.at[m] if src is None else src, dst_ref=sig.at[m],
            send_sem=sig_send.at[1, t], recv_sem=sig_recv.at[1, t],
            device_id=(en, down), device_id_type=MESH,
        )

    def columns(m):
        return pl.ds(pl.multiple_of(m * BS, BS), BS)

    def halo(t):
        copies = []
        for side, (dev, src_row, dst_row) in enumerate(
            ((up, rows - HALO, 0), (down, 0, rows + HALO))
        ):
            for which, m in enumerate((at_up(dev, t), at_down(dev, t))):
                copies.append(
                    pltpu.make_async_remote_copy(
                        src_ref=green.at[:, pl.ds(src_row, HALO), columns(m)],
                        dst_ref=ext.at[:, pl.ds(dst_row, HALO), columns(m)],
                        send_sem=halo_send.at[2 * side + which, t],
                        recv_sem=halo_recv.at[2 * side + which, t],
                        device_id=(en, dev), device_id_type=MESH,
                    )
                )
        return copies

    sig_up(1, sigma.at[0]).start()
    sig_down(1, sigma.at[1]).start()
    for copy in halo(0) + halo(1):
        copy.start()

    own_slab.wait()
    own_nbt.wait()
    pairs = slab.shape[1]
    degree = nbt.shape[0]
    pick = (iota((pairs, BS), 0) == en * degree + iota((pairs, BS), 1) // W).astype(F32)
    zed[...] = jnp.dot(slab_v[...], pick, preferred_element_type=F32, precision=HIGHEST)
    for c in range(3):
        for j in range(W):
            dlane[c * W + j] = zed[pl.ds(c * 64 + j, W, stride=W), :]
    atoms = rows // W
    near = jnp.where(iota((degree, atoms), 1) == en, nbt_v[...].astype(F32), 0.0)
    near = jnp.sum(near, axis=1, keepdims=True)
    off = jnp.where(
        iota((degree, BS), 0) == iota((degree, BS), 1) // W,
        jnp.broadcast_to(near, (degree, BS)), 0.0,
    )
    off = jnp.sum(off, axis=0, keepdims=True) - (me * atoms + en).astype(F32)
    place = off + 8.0 - (off > 0.0).astype(F32)
    place = jnp.broadcast_to(place, (W, BS))
    lane_l = iota((W, BS), 1) % W
    for c in range(3):
        v = jnp.zeros((W, BS), F32)
        for i in range(W):
            v = jnp.where(lane_l == i, zed[pl.ds(c * 64 + i * W, W), :], v)
        for d in range(2 * W):
            bd[pl.ds(d * W, W), pl.ds(c * BS, BS)] = jnp.where(place == float(d), v, 0.0)
    delta = iota((ne, ne), 1) - iota((ne, ne), 0)
    k = jnp.zeros((ne, ne), F32)
    for q in range(shift.shape[0]):
        k = k + jnp.where(delta == shift[q], weight[0, q], 0.0)
        k = k + jnp.where(delta == -shift[q], weight[1, q], 0.0)
    kmat[...] = k

    acc[...] = jnp.zeros_like(acc)
    own_sigma.wait()
    own_green.wait()

    def block(m):
        cols = columns(m)
        x = jnp.concatenate([ext[0, :, cols], ext[1, :, cols]], axis=1)
        xh, xl = split(x)
        sr, si = sig[m, 0], sig[m, 1]
        w = jnp.concatenate(
            [jnp.concatenate([sr, si], axis=1), jnp.concatenate([-si, sr], axis=1)], axis=0
        )
        wh, wl = split(w)
        ph, pq = split(dot(xh, wh) + (dot(xh, wl) + dot(xl, wh)))

        def stacked(v):
            return jnp.concatenate(
                [v, jnp.concatenate([v[:, BS:], -v[:, :BS]], axis=1)], axis=0
            )

        for h in range(2):
            lo, c0 = h * half_rows, h * 2 * HALO
            lh = stacked(ph[lo:lo + half_rows])
            lq = stacked(pq[lo:lo + half_rows])
            bh, bq = xh[c0:c0 + 256], xl[c0:c0 + 256]
            acc[h] += dot_nt(lh, bh) + (dot_nt(lh, bq) + dot_nt(lq, bh))

    def step(t, carry):
        @pl.when(t > 0)
        def _():
            sig_up(t).wait_recv()
            sig_down(t).wait_recv()

        @pl.when((t > 0) & (t < LEVELS - 1))
        def _():
            sig_up(t + 1).start()
            sig_down(t + 1).start()
            for copy in halo(t + 1):
                copy.start()

        for copy in halo(t):
            copy.wait_recv()
        first, second = at_up(me, t), at_down(me, t)

        def inner(u, c):
            block(first + u * (second - first))
            return c

        lax.fori_loop(0, 2, inner, 0)
        return carry

    lax.fori_loop(0, LEVELS, step, 0)

    lane = iota((W, BS), 1)

    def extract(h, i):
        s = ((64 if h == 0 else 224) - 8 * i) % 256
        s2 = (s - 8) % 256
        for z in range(2):
            x = acc[h, pl.ds(z * half_rows + 8 * i, W), :]
            y1 = pltpu.roll(x, s, 1)[:, :BS] if s else x[:, :BS]
            y2 = pltpu.roll(x, s2, 1)[:, :BS] if s2 else x[:, :BS]
            bx[h * 20 + i, pl.ds(z * W, W), :] = jnp.where(lane < 64, y1, y2)

    for i in range(4):
        extract(0, i)
        extract(1, 16 + i)
    to_down = pltpu.make_async_remote_copy(
        src_ref=bx.at[pl.ds(0, 4)], dst_ref=xin.at[1],
        send_sem=x_send.at[1], recv_sem=x_recv.at[1],
        device_id=(en, down), device_id_type=MESH,
    )
    to_up = pltpu.make_async_remote_copy(
        src_ref=bx.at[pl.ds(atoms + 4, 4)], dst_ref=xin.at[0],
        send_sem=x_send.at[0], recv_sem=x_recv.at[0],
        device_id=(en, up), device_id_type=MESH,
    )
    to_down.start()
    to_up.start()
    for i in range(16):
        extract(0, 4 + i)
        extract(1, i)
    to_down.wait_recv()
    to_up.wait_recv()
    lane2 = iota((2 * W, BS), 1)
    for a in range(4):
        bx[4 + a] = jnp.where(lane2 < 8 * (4 - a), xin[0, a], bx[4 + a])
        last = atoms + a
        bx[last] = jnp.where(lane2 >= 64 + 8 * (7 - a), xin[1, a], bx[last])

    own_rows = pl.ds(pl.multiple_of(en * 16, 16), 16)

    def there(d):
        return lax.rem(en + d, ne)

    def back(d):
        return lax.rem(en + ne - d, ne)

    def spread(d):
        to = there(d)
        return pltpu.make_async_remote_copy(
            src_ref=bx.at[4 + to], dst_ref=rcv.at[own_rows, :],
            send_sem=a_send.at[d], recv_sem=a_recv.at[d],
            device_id=(to, me), device_id_type=MESH,
        )

    def arrive(d):
        source = pl.ds(pl.multiple_of(back(d) * 16, 16), 16)
        return pltpu.make_async_remote_copy(
            src_ref=bx.at[4 + there(d)], dst_ref=rcv.at[source, :],
            send_sem=a_send.at[d], recv_sem=a_recv.at[d],
            device_id=(there(d), me), device_id_type=MESH,
        )

    def start_spread(d, carry):
        spread(d).start()
        return carry

    lax.fori_loop(1, ne, start_spread, 0)
    rcv[own_rows, :] = bx[4 + en]

    def wait_spread(d, carry):
        arrive(d).wait_recv()
        return carry

    lax.fori_loop(1, ne, wait_spread, 0)

    xs = jnp.concatenate([rcv[pl.ds(r, ne, stride=16), :] for r in range(16)], axis=1)
    ys = jnp.dot(kmat[...], xs, preferred_element_type=F32, precision=HIGHEST)
    for r in range(16):
        smeared[pl.ds(r, ne, stride=16), :] = ys[:, r * BS:(r + 1) * BS]
    bh, bq = split(bd[...])
    sh, sq = split(smeared[...])
    half[...] = dot(sh, bh) + (dot(sh, bq) + dot(sq, bh))

    def conjugate(e, carry):
        for z in range(2):
            base = pl.multiple_of(e * 16 + z * 8, 8)
            total = jnp.zeros((W, BS), F32)
            for c in range(3):
                block_t = half[pl.ds(base, W), pl.ds(c * BS, BS)]
                for j in range(W):
                    row = jnp.broadcast_to(block_t[j:j + 1, :], (W, BS))
                    total = total + dlane[c * W + j] * row
            done[pl.ds(base, W), :] = total
        return carry

    lax.fori_loop(0, ne, conjugate, 0, unroll=2)

    def back_home(d):
        to = there(d)
        return pltpu.make_async_remote_copy(
            src_ref=done.at[pl.ds(pl.multiple_of(to * 16, 16), 16), :],
            dst_ref=out.at[own_rows, :],
            send_sem=b_send.at[d], recv_sem=b_recv.at[d],
            device_id=(to, me), device_id_type=MESH,
        )

    def home_arrive(d):
        source = pl.ds(pl.multiple_of(back(d) * 16, 16), 16)
        return pltpu.make_async_remote_copy(
            src_ref=done.at[pl.ds(pl.multiple_of(there(d) * 16, 16), 16), :],
            dst_ref=out.at[source, :],
            send_sem=b_send.at[d], recv_sem=b_recv.at[d],
            device_id=(there(d), me), device_id_type=MESH,
        )

    def start_home(d, carry):
        back_home(d).start()
        return carry

    lax.fori_loop(1, ne, start_home, 0)
    keep = pltpu.make_async_copy(done.at[own_rows, :], out.at[own_rows, :], loc_sem.at[0])
    keep.start()

    to_down.wait_send()
    to_up.wait_send()

    def drain_ring(t, carry):
        sig_up(t).wait_send()
        sig_down(t).wait_send()
        return carry

    lax.fori_loop(1, LEVELS, drain_ring, 0)

    def drain_halo(t, carry):
        for copy in halo(t):
            copy.wait_send()
        return carry

    lax.fori_loop(0, LEVELS, drain_halo, 0)

    def finish(d, carry):
        spread(d).wait_send()
        home_arrive(d).wait_recv()
        back_home(d).wait_send()
        return carry

    lax.fori_loop(1, ne, finish, 0)
    keep.wait()


def order_kernel(x_ref, o_ref):
    n = 64
    row, blk = iota((n, BS), 0) % 16, iota((n, BS), 1) // W

    def chunk(c, carry):
        x = x_ref[pl.ds(pl.multiple_of(c * n, n), n), :]
        for b in (1, 2, 4, 8):
            rb, lb = (row // b) % 2, (blk // b) % 2
            upward = pltpu.roll(pltpu.roll(x, n - b, 0), W * b, 1)
            downward = pltpu.roll(pltpu.roll(x, b, 0), BS - W * b, 1)
            x = jnp.where(rb == lb, x, jnp.where(rb == 0, upward, downward))
        o_ref[pl.ds(pl.multiple_of(c * n, n), n), :] = x
        return carry

    lax.fori_loop(0, x_ref.shape[0] // n, chunk, 0)


def per_device(green, sigma, neighbours, phonon_shift, phonon_weight, dham):
    ne = lax.axis_size("energy")
    rows, cols = green.shape[2], green.shape[3]
    atoms, degree = neighbours.shape
    pairs = atoms * degree
    half_rows = rows // 2 + HALO
    slab = dham.transpose(1, 2, 3, 0).reshape(192, pairs)
    anyspec = pl.BlockSpec(memory_space=pl.ANY)
    smem = pl.BlockSpec(memory_space=pltpu.SMEM)
    dma = pltpu.SemaphoreType.DMA
    banded = pl.pallas_call(
        functools.partial(main_kernel, ne),
        out_shape=jax.ShapeDtypeStruct((pairs, BS), F32),
        in_specs=[anyspec, anyspec, anyspec, anyspec, smem, smem],
        out_specs=anyspec,
        scratch_shapes=[
            pltpu.VMEM((2, rows + 2 * HALO, cols), F32),
            pltpu.VMEM((cols // BS, 2, BS, BS), F32),
            pltpu.VMEM((2, 2 * half_rows, 256), F32),
            pltpu.VMEM((atoms + 8, 2 * W, BS), F32),
            pltpu.VMEM((2, 4, 2 * W, BS), F32),
            pltpu.VMEM((ne * 16, BS), F32),
            pltpu.VMEM((ne * 16, BS), F32),
            pltpu.VMEM((ne * 16, 3 * BS), F32),
            pltpu.VMEM((ne * 16, BS), F32),
            pltpu.VMEM((192, pairs), F32),
            pltpu.VMEM((degree, atoms), jnp.int32),
            pltpu.VMEM((192, BS), F32),
            pltpu.VMEM((24, W, BS), F32),
            pltpu.VMEM((BS, 3 * BS), F32),
            pltpu.VMEM((ne, ne), F32),
            dma((4,)),
            dma((2, LEVELS)), dma((2, LEVELS)),
            dma((4, LEVELS)), dma((4, LEVELS)),
            dma((2,)), dma((2,)),
            dma((ne,)), dma((ne,)),
            dma((ne,)), dma((ne,)),
        ],
        compiler_params=pltpu.CompilerParams(
            collective_id=0, has_side_effects=True, vmem_limit_bytes=64_000_000
        ),
        name="lesser",
    )(green[0], sigma[0], slab, neighbours.T, phonon_shift, phonon_weight)
    result = pl.pallas_call(
        order_kernel,
        out_shape=jax.ShapeDtypeStruct((pairs, BS), F32),
        in_specs=[pl.BlockSpec(memory_space=pltpu.VMEM)],
        out_specs=pl.BlockSpec(memory_space=pltpu.VMEM),
        name="order",
    )(banded)
    return result[None]


def solution(mesh):
    return jax.shard_map(
        per_device,
        mesh=mesh,
        in_specs=(
            P("energy", None, "orb", None),
            P("energy", "orb", None, None, None),
            P("orb", None),
            P(),
            P(),
            P("orb", None, None, None),
        ),
        out_specs=P("energy", "orb", None),
        check_vma=False,
    )
```

profile of v0, /device:TPU:1, one launch (start us, length us, event | category | flops | bytes accessed | tf_op | source)
XLA Modules:
  0.0 75.4 jit_solution(3305895566641374275)
XLA Ops:
  0.0 71.2 %lesser.1.x_ref = f32[512,128]{1,0:T(8,128)} custom-call(f32[2,256,2048]{2,1,0:T(8,128)} %bitcast.7, f32[2,2,128,128]{3,2,1,0:T(8,128)} %bitcast.9, f32[192,512]{1,0:T(8,128)} %bitcast.8, s32[16,32]{1,0:T(8,128)} %bitcast.10, s32[6]{0:T(128)} %shift.1, f32[2,6]{1,0:T(2,128)} %weight.1), custom_call_target="tpu_custom_call" | custom-call | tf_op jit(solution)/shard_map/lesser/pallas_call | solution.py:381
  71.2 4.2 %order.1 = f32[512,128]{1,0:T(8,128)} custom-call(f32[512,128]{1,0:T(8,128)} %lesser.1.x_ref), custom_call_target="tpu_custom_call" | custom-call | tf_op jit(solution)/shard_map/order/pallas_call | solution.py:414
where the time goes:
time: 75.5 us; the launch traced here: 75.4 us
  Pallas kernels  75.4 us (100%)
    pallas_call x1, Pallas kernels, per_device(): pl.pallas_call(functools.partial(main_kernel, ne), out_shape=jax.ShapeDty...  71.2 us
    pallas_call x1, Pallas kernels, per_device(): pl.pallas_call(order_kernel, out_shape=jax.ShapeDtypeStruct((pairs, BS),...  4.19 us

commit v1 on v0

--- a/solution.py
+++ b/solution.py
@@ -36,7 +36,7 @@
 
 def main_kernel(
     ne, green, sigma, slab, nbt, shift, weight, out,
-    ext, sig, acc, bx, xin, rcv, smeared, half, done, slab_v, nbt_v, zed, dlane, bd, kmat,
+    ext, sig, acc, bx, xin, rcv, half, done, slab_v, nbt_v, zed, bd, kmat,
     loc_sem, sig_send, sig_recv, halo_send, halo_recv, x_send, x_recv,
     a_send, a_recv, b_send, b_recv,
 ):
@@ -67,64 +67,12 @@
     own_nbt.start()
     own_sigma.start()
     own_green.start()
-    pl.semaphore_wait(barrier, ne + 1)
-
-    def at_up(dev, t):
-        return 2 * lax.rem(dev - t + 2 * LEVELS, LEVELS)
-
-    def at_down(dev, t):
-        return 2 * lax.rem(dev + t, LEVELS) + 1
-
-    def sig_up(t, src=None):
-        m = at_up(up, t)
-        return pltpu.make_async_remote_copy(
-            src_ref=sig.at[m] if src is None else src, dst_ref=sig.at[m],
-            send_sem=sig_send.at[0, t], recv_sem=sig_recv.at[0, t],
-            device_id=(en, up), device_id_type=MESH,
-        )
-
-    def sig_down(t, src=None):
-        m = at_down(down, t)
-        return pltpu.make_async_remote_copy(
-            src_ref=sig.at[m] if src is None else src, dst_ref=sig.at[m],
-            send_sem=sig_send.at[1, t], recv_sem=sig_recv.at[1, t],
-            device_id=(en, down), device_id_type=MESH,
-        )
-
-    def columns(m):
-        return pl.ds(pl.multiple_of(m * BS, BS), BS)
-
-    def halo(t):
-        copies = []
-        for side, (dev, src_row, dst_row) in enumerate(
-            ((up, rows - HALO, 0), (down, 0, rows + HALO))
-        ):
-            for which, m in enumerate((at_up(dev, t), at_down(dev, t))):
-                copies.append(
-                    pltpu.make_async_remote_copy(
-                        src_ref=green.at[:, pl.ds(src_row, HALO), columns(m)],
-                        dst_ref=ext.at[:, pl.ds(dst_row, HALO), columns(m)],
-                        send_sem=halo_send.at[2 * side + which, t],
-                        recv_sem=halo_recv.at[2 * side + which, t],
-                        device_id=(en, dev), device_id_type=MESH,
-                    )
-                )
-        return copies
-
-    sig_up(1, sigma.at[0]).start()
-    sig_down(1, sigma.at[1]).start()
-    for copy in halo(0) + halo(1):
-        copy.start()
-
     own_slab.wait()
     own_nbt.wait()
     pairs = slab.shape[1]
     degree = nbt.shape[0]
     pick = (iota((pairs, BS), 0) == en * degree + iota((pairs, BS), 1) // W).astype(F32)
     zed[...] = jnp.dot(slab_v[...], pick, preferred_element_type=F32, precision=HIGHEST)
-    for c in range(3):
-        for j in range(W):
-            dlane[c * W + j] = zed[pl.ds(c * 64 + j, W, stride=W), :]
     atoms = rows // W
     near = jnp.where(iota((degree, atoms), 1) == en, nbt_v[...].astype(F32), 0.0)
     near = jnp.sum(near, axis=1, keepdims=True)
@@ -148,8 +96,45 @@
         k = k + jnp.where(delta == shift[q], weight[0, q], 0.0)
         k = k + jnp.where(delta == -shift[q], weight[1, q], 0.0)
     kmat[...] = k
-
     acc[...] = jnp.zeros_like(acc)
+    pl.semaphore_wait(barrier, ne + 1)
+
+    def at_up(dev, t):
+        return 2 * lax.rem(dev - t + 2 * LEVELS, LEVELS)
+
+    def at_down(dev, t):
+        return 2 * lax.rem(dev + t, LEVELS) + 1
+
+    def ring(side, t, c, src=None):
+        dev = down if side else up
+        m = (at_down if side else at_up)(dev, t)
+        return pltpu.make_async_remote_copy(
+            src_ref=sig.at[m, c] if src is None else src, dst_ref=sig.at[m, c],
+            send_sem=sig_send.at[2 * side + c, t], recv_sem=sig_recv.at[2 * side + c, t],
+            device_id=(en, dev), device_id_type=MESH,
+        )
+
+    def columns(m):
+        return pl.ds(pl.multiple_of(m * BS, BS), BS)
+
+    def halo(side, t, c):
+        dev, src_row, dst_row = ((up, rows - HALO, 0), (down, 0, rows + HALO))[side]
+        m = (at_down if c else at_up)(dev, t)
+        return pltpu.make_async_remote_copy(
+            src_ref=green.at[:, pl.ds(src_row, HALO), columns(m)],
+            dst_ref=ext.at[:, pl.ds(dst_row, HALO), columns(m)],
+            send_sem=halo_send.at[2 * side + c, t], recv_sem=halo_recv.at[2 * side + c, t],
+            device_id=(en, dev), device_id_type=MESH,
+        )
+
+    for c in range(2):
+        for side in range(2):
+            ring(side, 1, c, sigma.at[side, c]).start()
+    for t in range(2):
+        for c in range(2):
+            for side in range(2):
+                halo(side, t, c).start()
+
     own_sigma.wait()
     own_green.wait()
 
@@ -177,30 +162,27 @@
             acc[h] += dot_nt(lh, bh) + (dot_nt(lh, bq) + dot_nt(lq, bh))
 
     def step(t, carry):
-        @pl.when(t > 0)
-        def _():
-            sig_up(t).wait_recv()
-            sig_down(t).wait_recv()
-
-        @pl.when((t > 0) & (t < LEVELS - 1))
-        def _():
-            sig_up(t + 1).start()
-            sig_down(t + 1).start()
-            for copy in halo(t + 1):
-                copy.start()
-
-        for copy in halo(t):
-            copy.wait_recv()
-        first, second = at_up(me, t), at_down(me, t)
-
-        def inner(u, c):
-            block(first + u * (second - first))
-            return c
-
-        lax.fori_loop(0, 2, inner, 0)
-        return carry
-
-    lax.fori_loop(0, LEVELS, step, 0)
+        for c in range(2):
+            for side in range(2):
+                @pl.when(t < LEVELS)
+                def _():
+                    ring(side, t, c).wait_recv()
+
+                @pl.when(t < LEVELS - 1)
+                def _():
+                    ring(side, t + 1, c).start()
+
+            @pl.when(t < LEVELS - 1)
+            def _():
+                for side in range(2):
+                    halo(side, t + 1, c).start()
+
+            for side in range(2):
+                halo(side, t - 1, c).wait_recv()
+            block((at_down if c else at_up)(me, t - 1))
+        return carry
+
+    lax.fori_loop(1, LEVELS + 1, step, 0)
 
     lane = iota((W, BS), 1)
 
@@ -231,6 +213,45 @@
     for i in range(16):
         extract(0, 4 + i)
         extract(1, i)
+
+    own_rows = pl.ds(pl.multiple_of(en * 16, 16), 16)
+
+    def there(d):
+        return lax.rem(en + d, ne)
+
+    def back(d):
+        return lax.rem(en + ne - d, ne)
+
+    def spread(d):
+        to = there(d)
+        return pltpu.make_async_remote_copy(
+            src_ref=bx.at[4 + to], dst_ref=rcv.at[own_rows, :],
+            send_sem=a_send.at[d], recv_sem=a_recv.at[d],
+            device_id=(to, me), device_id_type=MESH,
+        )
+
+    def arrive(d):
+        source = pl.ds(pl.multiple_of(back(d) * 16, 16), 16)
+        return pltpu.make_async_remote_copy(
+            src_ref=bx.at[4 + there(d)], dst_ref=rcv.at[source, :],
+            send_sem=a_send.at[d], recv_sem=a_recv.at[d],
+            device_id=(there(d), me), device_id_type=MESH,
+        )
+
+    def start_spread(edge):
+        def one(d, carry):
+            to = there(d)
+            at_edge = (to < 4) | (to >= atoms - 4)
+
+            @pl.when(at_edge if edge else jnp.logical_not(at_edge))
+            def _():
+                spread(d).start()
+
+            return carry
+
+        lax.fori_loop(1, ne, one, 0)
+
+    start_spread(False)
     to_down.wait_recv()
     to_up.wait_recv()
     lane2 = iota((2 * W, BS), 1)
@@ -238,36 +259,7 @@
         bx[4 + a] = jnp.where(lane2 < 8 * (4 - a), xin[0, a], bx[4 + a])
         last = atoms + a
         bx[last] = jnp.where(lane2 >= 64 + 8 * (7 - a), xin[1, a], bx[last])
-
-    own_rows = pl.ds(pl.multiple_of(en * 16, 16), 16)
-
-    def there(d):
-        return lax.rem(en + d, ne)
-
-    def back(d):
-        return lax.rem(en + ne - d, ne)
-
-    def spread(d):
-        to = there(d)
-        return pltpu.make_async_remote_copy(
-            src_ref=bx.at[4 + to], dst_ref=rcv.at[own_rows, :],
-            send_sem=a_send.at[d], recv_sem=a_recv.at[d],
-            device_id=(to, me), device_id_type=MESH,
-        )
-
-    def arrive(d):
-        source = pl.ds(pl.multiple_of(back(d) * 16, 16), 16)
-        return pltpu.make_async_remote_copy(
-            src_ref=bx.at[4 + there(d)], dst_ref=rcv.at[source, :],
-            send_sem=a_send.at[d], recv_sem=a_recv.at[d],
-            device_id=(there(d), me), device_id_type=MESH,
-        )
-
-    def start_spread(d, carry):
-        spread(d).start()
-        return carry
-
-    lax.fori_loop(1, ne, start_spread, 0)
+    start_spread(True)
     rcv[own_rows, :] = bx[4 + en]
 
     def wait_spread(d, carry):
@@ -278,25 +270,40 @@
 
     xs = jnp.concatenate([rcv[pl.ds(r, ne, stride=16), :] for r in range(16)], axis=1)
     ys = jnp.dot(kmat[...], xs, preferred_element_type=F32, precision=HIGHEST)
-    for r in range(16):
-        smeared[pl.ds(r, ne, stride=16), :] = ys[:, r * BS:(r + 1) * BS]
+    yh, yq = split(jnp.concatenate([ys[:, r * BS:(r + 1) * BS] for r in range(16)], axis=0))
     bh, bq = split(bd[...])
-    sh, sq = split(smeared[...])
-    half[...] = dot(sh, bh) + (dot(sh, bq) + dot(sq, bh))
-
-    def conjugate(e, carry):
+    half[...] = dot(yh, bh) + (dot(yh, bq) + dot(yq, bh))
+
+    def conjugate(tile, carry):
+        v = []
         for z in range(2):
-            base = pl.multiple_of(e * 16 + z * 8, 8)
-            total = jnp.zeros((W, BS), F32)
-            for c in range(3):
-                block_t = half[pl.ds(base, W), pl.ds(c * BS, BS)]
-                for j in range(W):
-                    row = jnp.broadcast_to(block_t[j:j + 1, :], (W, BS))
-                    total = total + dlane[c * W + j] * row
-            done[pl.ds(base, W), :] = total
-        return carry
-
-    lax.fori_loop(0, ne, conjugate, 0, unroll=2)
+            t = [
+                half[
+                    pl.ds(pl.multiple_of((z * W + j) * ne + tile * W, W), W),
+                    pl.ds(c * BS, BS),
+                ]
+                for c in range(3) for j in range(W)
+            ]
+            for i in range(W):
+                total = jnp.zeros((W, BS), F32)
+                for c in range(3):
+                    for j in range(W):
+                        row = jnp.broadcast_to(zed[pl.ds(c * 64 + i * W + j, 1), :], (W, BS))
+                        total = total + row * t[c * W + j]
+                v.append(total)
+        for b in (1, 2, 4, 8):
+            keep_low = (lane // (W * b)) % 2 == 0
+            new = list(v)
+            for r in range(16):
+                if not r & b:
+                    new[r] = jnp.where(keep_low, v[r], pltpu.roll(v[r + b], W * b, 1))
+                    new[r + b] = jnp.where(keep_low, pltpu.roll(v[r], BS - W * b, 1), v[r + b])
+            v = new
+        for k in range(16):
+            done[pl.ds(tile * BS + k, W, stride=16), :] = v[k]
+        return carry
+
+    lax.fori_loop(0, ne // W, conjugate, 0)
 
     def back_home(d):
         to = there(d)
@@ -328,15 +335,17 @@
     to_up.wait_send()
 
     def drain_ring(t, carry):
-        sig_up(t).wait_send()
-        sig_down(t).wait_send()
+        for c in range(2):
+            for side in range(2):
+                ring(side, t, c).wait_send()
         return carry
 
     lax.fori_loop(1, LEVELS, drain_ring, 0)
 
     def drain_halo(t, carry):
-        for copy in halo(t):
-            copy.wait_send()
+        for c in range(2):
+            for side in range(2):
+                halo(side, t, c).wait_send()
         return carry
 
     lax.fori_loop(0, LEVELS, drain_halo, 0)
@@ -349,23 +358,6 @@
 
     lax.fori_loop(1, ne, finish, 0)
     keep.wait()
-
-
-def order_kernel(x_ref, o_ref):
-    n = 64
-    row, blk = iota((n, BS), 0) % 16, iota((n, BS), 1) // W
-
-    def chunk(c, carry):
-        x = x_ref[pl.ds(pl.multiple_of(c * n, n), n), :]
-        for b in (1, 2, 4, 8):
-            rb, lb = (row // b) % 2, (blk // b) % 2
-            upward = pltpu.roll(pltpu.roll(x, n - b, 0), W * b, 1)
-            downward = pltpu.roll(pltpu.roll(x, b, 0), BS - W * b, 1)
-            x = jnp.where(rb == lb, x, jnp.where(rb == 0, upward, downward))
-        o_ref[pl.ds(pl.multiple_of(c * n, n), n), :] = x
-        return carry
-
-    lax.fori_loop(0, x_ref.shape[0] // n, chunk, 0)
 
 
 def per_device(green, sigma, neighbours, phonon_shift, phonon_weight, dham):
@@ -390,17 +382,15 @@
             pltpu.VMEM((atoms + 8, 2 * W, BS), F32),
             pltpu.VMEM((2, 4, 2 * W, BS), F32),
             pltpu.VMEM((ne * 16, BS), F32),
-            pltpu.VMEM((ne * 16, BS), F32),
             pltpu.VMEM((ne * 16, 3 * BS), F32),
             pltpu.VMEM((ne * 16, BS), F32),
             pltpu.VMEM((192, pairs), F32),
             pltpu.VMEM((degree, atoms), jnp.int32),
             pltpu.VMEM((192, BS), F32),
-            pltpu.VMEM((24, W, BS), F32),
             pltpu.VMEM((BS, 3 * BS), F32),
             pltpu.VMEM((ne, ne), F32),
             dma((4,)),
-            dma((2, LEVELS)), dma((2, LEVELS)),
+            dma((4, LEVELS)), dma((4, LEVELS)),
             dma((4, LEVELS)), dma((4, LEVELS)),
             dma((2,)), dma((2,)),
             dma((ne,)), dma((ne,)),
@@ -411,14 +401,7 @@
         ),
         name="lesser",
     )(green[0], sigma[0], slab, neighbours.T, phonon_shift, phonon_weight)
-    result = pl.pallas_call(
-        order_kernel,
-        out_shape=jax.ShapeDtypeStruct((pairs, BS), F32),
-        in_specs=[pl.BlockSpec(memory_space=pltpu.VMEM)],
-        out_specs=pl.BlockSpec(memory_space=pltpu.VMEM),
-        name="order",
-    )(banded)
-    return result[None]
+    return banded[None]
 
 
 def solution(mesh):

time: 75.5 us -> 67.4 us (0.89)
  Pallas kernels: 75.4 us -> 65.6 us
  local copies, waits for them, and re-layouts: 0 us -> 1.67 us
    pallas_call x1, Pallas kernels: 71.2 us -> 65.6 us  [per_device(): pl.pallas_call(functools.partial(main_kernel, ne), out_shape=jax.ShapeDty...]
    pallas_call x1 -> x0, Pallas kernels: 4.19 us -> none  [per_device(): pl.pallas_call(order_kernel, out_shape=jax.ShapeDtypeStruct((pairs, BS),...]
    unnamed x0 -> x1, local copies, waits for them, and re-layouts: none -> 1.67 us
where the time goes in v1:
time: 67.4 us; the launch traced here: 67.3 us
  Pallas kernels  65.6 us (97%)
  local copies, waits for them, and re-layouts  1.67 us (2%)
    pallas_call x1, Pallas kernels, per_device(): pl.pallas_call(functools.partial(main_kernel, ne), out_shape=jax.ShapeDty...  65.6 us
    unnamed x1, local copies, waits for them, and re-layouts  1.67 us

profile of v1, /device:TPU:1, one launch (start us, length us, event | category | flops | bytes accessed | tf_op | source)
XLA Modules:
  0.0 67.3 jit_solution(18142305955713791936)
XLA Ops:
  0.0 65.6 %lesser.1 = f32[512,128]{1,0:T(8,128)} custom-call(f32[2,256,2048]{2,1,0:T(8,128)} %bitcast.7, f32[2,2,128,128]{3,2,1,0:T(8,128)} %bitcast.10, f32[192,512]{1,0:T(8,128)} %bitcast.9, s32[16,32]{1,0:T(8,128)} %bitcast.11, s32[6]{0:T(128)} %shift.1, f32[2,6]{1,0:T(2,128)} %weight.1), custom_call_target="tpu_custom_call" | custom-call | tf_op jit(solution)/shard_map/lesser/pallas_call | solution.py:373
  65.6 1.7 %copy.8 = f32[1,512,128]{2,1,0:T(8,128)} copy(f32[1,512,128]{2,1,0:T(8,128)} %bitcast.8) | data formatting | bytes 524288

commit v2 on v1

--- a/solution.py
+++ b/solution.py
@@ -11,7 +11,12 @@
 BS = 128
 HALO = 32
 LEVELS = 8
+SIDE = 4
 MESH = pl.DeviceIdType.MESH
+FAR_FIRST = sorted(
+    ((dy, dx, dc) for dy in range(SIDE) for dx in range(SIDE) for dc in range(2) if dy or dx or dc),
+    key=lambda o: -(min(o[0], SIDE - o[0]) + min(o[1], SIDE - o[1])),
+)
 HIGHEST = lax.Precision.HIGHEST
 F32 = jnp.float32
 BF16 = jnp.bfloat16
@@ -36,7 +41,7 @@
 
 def main_kernel(
     ne, green, sigma, slab, nbt, shift, weight, out,
-    ext, sig, acc, bx, xin, rcv, half, done, slab_v, nbt_v, zed, bd, kmat,
+    ext, sig, acc, bx, xin, rcv, half, done, slab_v, nbt_v, zed, zexp, bd, kmat, known,
     loc_sem, sig_send, sig_recv, halo_send, halo_recv, x_send, x_recv,
     a_send, a_recv, b_send, b_recv,
 ):
@@ -47,17 +52,25 @@
     rows = green.shape[1]
     half_rows = rows // 2 + HALO
 
+    core, chip_x, chip_y = en % 2, en // 2 % SIDE, en // (2 * SIDE)
+
+    def moved(dy, dx, dc):
+        return (
+            (chip_y + dy + SIDE) % SIDE * SIDE + (chip_x + dx + SIDE) % SIDE
+        ) * 2 + (core + dc) % 2
+
     barrier = pltpu.get_barrier_semaphore()
     for z in (up, down):
         pl.semaphore_signal(barrier, inc=1, device_id=(en, z), device_id_type=MESH)
-
-    def greet(d, carry):
+    for step_to in ((0, 1, 0), (0, -1, 0), (1, 0, 0), (-1, 0, 0), (0, 0, 1)):
         pl.semaphore_signal(
-            barrier, inc=1, device_id=(lax.rem(en + d, ne), me), device_id_type=MESH
-        )
-        return carry
-
-    lax.fori_loop(1, ne, greet, 0)
+            barrier, inc=1, device_id=(moved(*step_to), me), device_id_type=MESH
+        )
+
+    def tell(r):
+        for sign in (1, -1):
+            to = moved(0, sign, 0) if r < 2 else moved(sign, 0, 0)
+            pl.semaphore_signal(known.at[r], inc=1, device_id=(to, me), device_id_type=MESH)
 
     own_green = pltpu.make_async_copy(green, ext.at[:, pl.ds(HALO, rows), :], loc_sem.at[0])
     own_sigma = pltpu.make_async_copy(sigma, sig.at[pl.ds(2 * me, 2)], loc_sem.at[1])
@@ -67,6 +80,45 @@
     own_nbt.start()
     own_sigma.start()
     own_green.start()
+    pl.semaphore_wait(barrier, 7)
+
+    def at_up(dev, t):
+        return 2 * lax.rem(dev - t + 2 * LEVELS, LEVELS)
+
+    def at_down(dev, t):
+        return 2 * lax.rem(dev + t, LEVELS) + 1
+
+    def ring(side, t, c, src=None):
+        dev = down if side else up
+        m = (at_down if side else at_up)(dev, t)
+        return pltpu.make_async_remote_copy(
+            src_ref=sig.at[m, c] if src is None else src, dst_ref=sig.at[m, c],
+            send_sem=sig_send.at[2 * side + c, t], recv_sem=sig_recv.at[2 * side + c, t],
+            device_id=(en, dev), device_id_type=MESH,
+        )
+
+    def columns(m):
+        return pl.ds(pl.multiple_of(m * BS, BS), BS)
+
+    def halo(side, t, c):
+        dev, src_row, dst_row = ((up, rows - HALO, 0), (down, 0, rows + HALO))[side]
+        m = (at_down if c else at_up)(dev, t)
+        return pltpu.make_async_remote_copy(
+            src_ref=green.at[:, pl.ds(src_row, HALO), columns(m)],
+            dst_ref=ext.at[:, pl.ds(dst_row, HALO), columns(m)],
+            send_sem=halo_send.at[2 * side + c, t], recv_sem=halo_recv.at[2 * side + c, t],
+            device_id=(en, dev), device_id_type=MESH,
+        )
+
+    for c in range(2):
+        for side in range(2):
+            ring(side, 1, c, sigma.at[side, c]).start()
+    for t in range(2):
+        for c in range(2):
+            for side in range(2):
+                halo(side, t, c).start()
+    tell(0)
+
     own_slab.wait()
     own_nbt.wait()
     pairs = slab.shape[1]
@@ -97,43 +149,14 @@
         k = k + jnp.where(delta == -shift[q], weight[1, q], 0.0)
     kmat[...] = k
     acc[...] = jnp.zeros_like(acc)
-    pl.semaphore_wait(barrier, ne + 1)
-
-    def at_up(dev, t):
-        return 2 * lax.rem(dev - t + 2 * LEVELS, LEVELS)
-
-    def at_down(dev, t):
-        return 2 * lax.rem(dev + t, LEVELS) + 1
-
-    def ring(side, t, c, src=None):
-        dev = down if side else up
-        m = (at_down if side else at_up)(dev, t)
-        return pltpu.make_async_remote_copy(
-            src_ref=sig.at[m, c] if src is None else src, dst_ref=sig.at[m, c],
-            send_sem=sig_send.at[2 * side + c, t], recv_sem=sig_recv.at[2 * side + c, t],
-            device_id=(en, dev), device_id_type=MESH,
-        )
-
-    def columns(m):
-        return pl.ds(pl.multiple_of(m * BS, BS), BS)
-
-    def halo(side, t, c):
-        dev, src_row, dst_row = ((up, rows - HALO, 0), (down, 0, rows + HALO))[side]
-        m = (at_down if c else at_up)(dev, t)
-        return pltpu.make_async_remote_copy(
-            src_ref=green.at[:, pl.ds(src_row, HALO), columns(m)],
-            dst_ref=ext.at[:, pl.ds(dst_row, HALO), columns(m)],
-            send_sem=halo_send.at[2 * side + c, t], recv_sem=halo_recv.at[2 * side + c, t],
-            device_id=(en, dev), device_id_type=MESH,
-        )
-
-    for c in range(2):
-        for side in range(2):
-            ring(side, 1, c, sigma.at[side, c]).start()
-    for t in range(2):
-        for c in range(2):
-            for side in range(2):
-                halo(side, t, c).start()
+
+    def widen(r, carry):
+        tile = zed[pl.ds(pl.multiple_of(r * W, W), W), :]
+        for j in range(W):
+            zexp[r * W + j] = jnp.broadcast_to(tile[j:j + 1, :], (W, BS))
+        return carry
+
+    lax.fori_loop(0, 24, widen, 0)
 
     own_sigma.wait()
     own_green.wait()
@@ -161,28 +184,41 @@
             bh, bq = xh[c0:c0 + 256], xl[c0:c0 + 256]
             acc[h] += dot_nt(lh, bh) + (dot_nt(lh, bq) + dot_nt(lq, bh))
 
+    def due(t, c):
+        for side in range(2):
+            halo(side, t, c).wait_recv()
+        block((at_down if c else at_up)(me, t))
+
     def step(t, carry):
         for c in range(2):
             for side in range(2):
-                @pl.when(t < LEVELS)
-                def _():
+                ring(side, t, c).wait_recv()
+                ring(side, t + 1, c).start()
+            for side in range(2):
+                halo(side, t + 1, c).start()
+            due(t - 1, c)
+        for r in range(4):
+            @pl.when(t == r + 1)
+            def _():
+                pl.semaphore_wait(known.at[r], 2)
+                if r < 3:
+                    tell(r + 1)
+        return carry
+
+    lax.fori_loop(1, LEVELS - 1, step, 0)
+
+    def last(t, carry):
+        @pl.when(t == LEVELS - 1)
+        def _():
+            for c in range(2):
+                for side in range(2):
                     ring(side, t, c).wait_recv()
 
-                @pl.when(t < LEVELS - 1)
-                def _():
-                    ring(side, t + 1, c).start()
-
-            @pl.when(t < LEVELS - 1)
-            def _():
-                for side in range(2):
-                    halo(side, t + 1, c).start()
-
-            for side in range(2):
-                halo(side, t - 1, c).wait_recv()
-            block((at_down if c else at_up)(me, t - 1))
+        due(t, 0)
+        due(t, 1)
         return carry
 
-    lax.fori_loop(1, LEVELS + 1, step, 0)
+    lax.fori_loop(LEVELS - 2, LEVELS, last, 0)
 
     lane = iota((W, BS), 1)
 
@@ -217,39 +253,32 @@
     own_rows = pl.ds(pl.multiple_of(en * 16, 16), 16)
 
     def there(d):
-        return lax.rem(en + d, ne)
+        return moved(*FAR_FIRST[d])
 
     def back(d):
-        return lax.rem(en + ne - d, ne)
-
-    def spread(d):
+        dy, dx, dc = FAR_FIRST[d]
+        return moved(-dy, -dx, dc)
+
+    def rows_of(e):
+        return pl.ds(pl.multiple_of(e * 16, 16), 16)
+
+    def spread(d, source=None):
         to = there(d)
         return pltpu.make_async_remote_copy(
-            src_ref=bx.at[4 + to], dst_ref=rcv.at[own_rows, :],
+            src_ref=bx.at[4 + to],
+            dst_ref=rcv.at[own_rows if source is None else rows_of(source), :],
             send_sem=a_send.at[d], recv_sem=a_recv.at[d],
             device_id=(to, me), device_id_type=MESH,
         )
 
-    def arrive(d):
-        source = pl.ds(pl.multiple_of(back(d) * 16, 16), 16)
-        return pltpu.make_async_remote_copy(
-            src_ref=bx.at[4 + there(d)], dst_ref=rcv.at[source, :],
-            send_sem=a_send.at[d], recv_sem=a_recv.at[d],
-            device_id=(there(d), me), device_id_type=MESH,
-        )
-
     def start_spread(edge):
-        def one(d, carry):
+        for d in range(ne - 1):
             to = there(d)
             at_edge = (to < 4) | (to >= atoms - 4)
 
             @pl.when(at_edge if edge else jnp.logical_not(at_edge))
             def _():
                 spread(d).start()
-
-            return carry
-
-        lax.fori_loop(1, ne, one, 0)
 
     start_spread(False)
     to_down.wait_recv()
@@ -262,35 +291,34 @@
     start_spread(True)
     rcv[own_rows, :] = bx[4 + en]
 
-    def wait_spread(d, carry):
-        arrive(d).wait_recv()
-        return carry
-
-    lax.fori_loop(1, ne, wait_spread, 0)
+    for d in range(ne - 1):
+        spread(d, back(d)).wait_recv()
 
     xs = jnp.concatenate([rcv[pl.ds(r, ne, stride=16), :] for r in range(16)], axis=1)
-    ys = jnp.dot(kmat[...], xs, preferred_element_type=F32, precision=HIGHEST)
+    xh, xq = split(xs)
+    kh, kq = split(kmat[...])
+    ys = dot(kh, xh) + (dot(kh, xq) + dot(kq, xh))
     yh, yq = split(jnp.concatenate([ys[:, r * BS:(r + 1) * BS] for r in range(16)], axis=0))
     bh, bq = split(bd[...])
     half[...] = dot(yh, bh) + (dot(yh, bq) + dot(yq, bh))
 
-    def conjugate(tile, carry):
+    def conjugate(tile):
         v = []
         for z in range(2):
             t = [
                 half[
-                    pl.ds(pl.multiple_of((z * W + j) * ne + tile * W, W), W),
+                    pl.ds((z * W + j) * ne + tile * W, W),
                     pl.ds(c * BS, BS),
                 ]
                 for c in range(3) for j in range(W)
             ]
             for i in range(W):
-                total = jnp.zeros((W, BS), F32)
+                total = [None, None]
                 for c in range(3):
                     for j in range(W):
-                        row = jnp.broadcast_to(zed[pl.ds(c * 64 + i * W + j, 1), :], (W, BS))
-                        total = total + row * t[c * W + j]
-                v.append(total)
+                        term = zexp[c * 64 + i * W + j] * t[c * W + j]
+                        total[j % 2] = term if total[j % 2] is None else total[j % 2] + term
+                v.append(total[0] + total[1])
         for b in (1, 2, 4, 8):
             keep_low = (lane // (W * b)) % 2 == 0
             new = list(v)
@@ -301,33 +329,21 @@
             v = new
         for k in range(16):
             done[pl.ds(tile * BS + k, W, stride=16), :] = v[k]
-        return carry
-
-    lax.fori_loop(0, ne // W, conjugate, 0)
-
-    def back_home(d):
+
+    for tile in range(ne // W):
+        conjugate(tile)
+
+    def back_home(d, source=None):
         to = there(d)
         return pltpu.make_async_remote_copy(
-            src_ref=done.at[pl.ds(pl.multiple_of(to * 16, 16), 16), :],
-            dst_ref=out.at[own_rows, :],
+            src_ref=done.at[rows_of(to), :],
+            dst_ref=out.at[own_rows if source is None else rows_of(source), :],
             send_sem=b_send.at[d], recv_sem=b_recv.at[d],
             device_id=(to, me), device_id_type=MESH,
         )
 
-    def home_arrive(d):
-        source = pl.ds(pl.multiple_of(back(d) * 16, 16), 16)
-        return pltpu.make_async_remote_copy(
-            src_ref=done.at[pl.ds(pl.multiple_of(there(d) * 16, 16), 16), :],
-            dst_ref=out.at[source, :],
-            send_sem=b_send.at[d], recv_sem=b_recv.at[d],
-            device_id=(there(d), me), device_id_type=MESH,
-        )
-
-    def start_home(d, carry):
+    for d in range(ne - 1):
         back_home(d).start()
-        return carry
-
-    lax.fori_loop(1, ne, start_home, 0)
     keep = pltpu.make_async_copy(done.at[own_rows, :], out.at[own_rows, :], loc_sem.at[0])
     keep.start()
 
@@ -350,13 +366,12 @@
 
     lax.fori_loop(0, LEVELS, drain_halo, 0)
 
-    def finish(d, carry):
+    for d in range(ne - 1):
         spread(d).wait_send()
-        home_arrive(d).wait_recv()
+    for d in range(ne - 1):
+        back_home(d, back(d)).wait_recv()
+    for d in range(ne - 1):
         back_home(d).wait_send()
-        return carry
-
-    lax.fori_loop(1, ne, finish, 0)
     keep.wait()
 
 
@@ -387,8 +402,10 @@
             pltpu.VMEM((192, pairs), F32),
             pltpu.VMEM((degree, atoms), jnp.int32),
             pltpu.VMEM((192, BS), F32),
+            pltpu.VMEM((192, W, BS), F32),
             pltpu.VMEM((BS, 3 * BS), F32),
             pltpu.VMEM((ne, ne), F32),
+            pltpu.SemaphoreType.REGULAR((4,)),
             dma((4,)),
             dma((4, LEVELS)), dma((4, LEVELS)),
             dma((4, LEVELS)), dma((4, LEVELS)),

time: 67.4 us -> 64 us (0.950)
  Pallas kernels: 65.6 us -> 62.2 us
    pallas_call x1, Pallas kernels: 65.6 us -> 62.2 us  [per_device(): pl.pallas_call(functools.partial(main_kernel, ne), out_shape=jax.ShapeDty...]
where the time goes in v2:
time: 64 us; the launch traced here: 63.9 us
  Pallas kernels  62.2 us (97%)
  local copies, waits for them, and re-layouts  1.67 us (3%)
    pallas_call x1, Pallas kernels, per_device(): pl.pallas_call(functools.partial(main_kernel, ne), out_shape=jax.ShapeDty...  62.2 us
    unnamed x1, local copies, waits for them, and re-layouts  1.67 us

profile of v2, /device:TPU:1, one launch (start us, length us, event | category | flops | bytes accessed | tf_op | source)
XLA Modules:
  0.0 63.9 jit_solution(15307716809945654193)
XLA Ops:
  0.0 62.2 %lesser.1 = f32[512,128]{1,0:T(8,128)} custom-call(f32[2,256,2048]{2,1,0:T(8,128)} %bitcast.7, f32[2,2,128,128]{3,2,1,0:T(8,128)} %bitcast.10, f32[192,512]{1,0:T(8,128)} %bitcast.9, s32[16,32]{1,0:T(8,128)} %bitcast.11, s32[6]{0:T(128)} %shift.1, f32[2,6]{1,0:T(2,128)} %weight.1), custom_call_target="tpu_custom_call" | custom-call | tf_op jit(solution)/shard_map/lesser/pallas_call | solution.py:388
  62.2 1.7 %copy.8 = f32[1,512,128]{2,1,0:T(8,128)} copy(f32[1,512,128]{2,1,0:T(8,128)} %bitcast.8) | data formatting | bytes 524288

commit v3 on v2

--- a/solution.py
+++ b/solution.py
@@ -22,6 +22,14 @@
 BF16 = jnp.bfloat16
 
 
+def atom_of(e):
+    return e // 2 + 16 * (e % 2)
+
+
+def device_of(a):
+    return 2 * (a % 16) + a // 16
+
+
 def split(x):
     high = x.astype(BF16)
     return high, (x - high.astype(F32)).astype(BF16)
@@ -41,8 +49,8 @@
 
 def main_kernel(
     ne, green, sigma, slab, nbt, shift, weight, out,
-    ext, sig, acc, bx, xin, rcv, half, done, slab_v, nbt_v, zed, zexp, bd, kmat, known,
-    loc_sem, sig_send, sig_recv, halo_send, halo_recv, x_send, x_recv,
+    ext, sig, acc, bx, pair, rcv, rcv_n, half, done, slab_v, nbt_v, zed, zexp, bd, kmat, known,
+    loc_sem, sig_send, sig_recv, halo_send, halo_recv, n_send, n_recv,
     a_send, a_recv, b_send, b_recv,
 ):
     en = lax.axis_index("energy")
@@ -50,6 +58,7 @@
     up = lax.rem(me + 1, LEVELS)
     down = lax.rem(me + LEVELS - 1, LEVELS)
     rows = green.shape[1]
+    mine = atom_of(en)
     half_rows = rows // 2 + HALO
 
     core, chip_x, chip_y = en % 2, en // 2 % SIDE, en // (2 * SIDE)
@@ -123,16 +132,16 @@
     own_nbt.wait()
     pairs = slab.shape[1]
     degree = nbt.shape[0]
-    pick = (iota((pairs, BS), 0) == en * degree + iota((pairs, BS), 1) // W).astype(F32)
+    pick = (iota((pairs, BS), 0) == mine * degree + iota((pairs, BS), 1) // W).astype(F32)
     zed[...] = jnp.dot(slab_v[...], pick, preferred_element_type=F32, precision=HIGHEST)
     atoms = rows // W
-    near = jnp.where(iota((degree, atoms), 1) == en, nbt_v[...].astype(F32), 0.0)
+    near = jnp.where(iota((degree, atoms), 1) == mine, nbt_v[...].astype(F32), 0.0)
     near = jnp.sum(near, axis=1, keepdims=True)
     off = jnp.where(
         iota((degree, BS), 0) == iota((degree, BS), 1) // W,
         jnp.broadcast_to(near, (degree, BS)), 0.0,
     )
-    off = jnp.sum(off, axis=0, keepdims=True) - (me * atoms + en).astype(F32)
+    off = jnp.sum(off, axis=0, keepdims=True) - (me * atoms + mine).astype(F32)
     place = off + 8.0 - (off > 0.0).astype(F32)
     place = jnp.broadcast_to(place, (W, BS))
     lane_l = iota((W, BS), 1) % W
@@ -234,24 +243,34 @@
     for i in range(4):
         extract(0, i)
         extract(1, 16 + i)
-    to_down = pltpu.make_async_remote_copy(
-        src_ref=bx.at[pl.ds(0, 4)], dst_ref=xin.at[1],
-        send_sem=x_send.at[1], recv_sem=x_recv.at[1],
-        device_id=(en, down), device_id_type=MESH,
-    )
-    to_up = pltpu.make_async_remote_copy(
-        src_ref=bx.at[pl.ds(atoms + 4, 4)], dst_ref=xin.at[0],
-        send_sem=x_send.at[0], recv_sem=x_recv.at[0],
-        device_id=(en, up), device_id_type=MESH,
-    )
-    to_down.start()
-    to_up.start()
+    own_rows = pl.ds(pl.multiple_of(en * 16, 16), 16)
+
+    def beside(n):
+        to, level = (atoms - 4 + n, down) if n < 4 else (n - 4, up)
+        return pltpu.make_async_remote_copy(
+            src_ref=pair.at[n], dst_ref=rcv_n.at[en],
+            send_sem=n_send.at[n], recv_sem=n_recv.at[en],
+            device_id=(device_of(to), level), device_id_type=MESH,
+        )
+
+    def from_beside(e):
+        return pltpu.make_async_remote_copy(
+            src_ref=pair.at[0], dst_ref=rcv_n.at[e],
+            send_sem=n_send.at[0], recv_sem=n_recv.at[e],
+            device_id=(en, up), device_id_type=MESH,
+        )
+
+    for n in range(4):
+        re, im = bx[n, :W], pltpu.roll(bx[n, W:], 96, 1)
+        pair[n] = jnp.where(lane >= 96, re, im)
+        re, im = bx[atoms + 4 + n, :W], pltpu.roll(bx[atoms + 4 + n, W:], 32, 1)
+        pair[4 + n] = jnp.where(lane < 32, re, im)
+    for n in range(8):
+        beside(n).start()
     for i in range(16):
         extract(0, 4 + i)
         extract(1, i)
 
-    own_rows = pl.ds(pl.multiple_of(en * 16, 16), 16)
-
     def there(d):
         return moved(*FAR_FIRST[d])
 
@@ -265,34 +284,35 @@
     def spread(d, source=None):
         to = there(d)
         return pltpu.make_async_remote_copy(
-            src_ref=bx.at[4 + to],
+            src_ref=bx.at[4 + atom_of(to)],
             dst_ref=rcv.at[own_rows if source is None else rows_of(source), :],
             send_sem=a_send.at[d], recv_sem=a_recv.at[d],
             device_id=(to, me), device_id_type=MESH,
         )
 
-    def start_spread(edge):
-        for d in range(ne - 1):
-            to = there(d)
-            at_edge = (to < 4) | (to >= atoms - 4)
-
-            @pl.when(at_edge if edge else jnp.logical_not(at_edge))
-            def _():
-                spread(d).start()
-
-    start_spread(False)
-    to_down.wait_recv()
-    to_up.wait_recv()
-    lane2 = iota((2 * W, BS), 1)
-    for a in range(4):
-        bx[4 + a] = jnp.where(lane2 < 8 * (4 - a), xin[0, a], bx[4 + a])
-        last = atoms + a
-        bx[last] = jnp.where(lane2 >= 64 + 8 * (7 - a), xin[1, a], bx[last])
-    start_spread(True)
-    rcv[own_rows, :] = bx[4 + en]
+    for d in range(ne - 1):
+        spread(d).start()
+    rcv[own_rows, :] = bx[4 + mine]
 
     for d in range(ne - 1):
         spread(d, back(d)).wait_recv()
+
+    @pl.when((mine < 4) | (mine >= atoms - 4))
+    def _():
+        def wait_beside(e, carry):
+            from_beside(e).wait_recv()
+            return carry
+
+        lax.fori_loop(0, ne, wait_beside, 0)
+        low = jnp.where(mine < 4, 8 * (4 - mine), 0)
+        high = jnp.where(mine >= atoms - 4, 64 + 8 * (7 + atoms - 4 - mine), BS)
+        take = (lane < low) | (lane >= high)
+        for e in range(ne):
+            re = rcv_n[e]
+            im = jnp.where(mine < 4, pltpu.roll(re, 96, 1), pltpu.roll(re, 32, 1))
+            for z, part in enumerate((re, im)):
+                r = pl.ds(16 * e + W * z, W)
+                rcv[r, :] = jnp.where(take, part, rcv[r, :])
 
     xs = jnp.concatenate([rcv[pl.ds(r, ne, stride=16), :] for r in range(16)], axis=1)
     xh, xq = split(xs)
@@ -337,18 +357,18 @@
         to = there(d)
         return pltpu.make_async_remote_copy(
             src_ref=done.at[rows_of(to), :],
-            dst_ref=out.at[own_rows if source is None else rows_of(source), :],
+            dst_ref=out.at[rows_of(mine if source is None else atom_of(source)), :],
             send_sem=b_send.at[d], recv_sem=b_recv.at[d],
             device_id=(to, me), device_id_type=MESH,
         )
 
     for d in range(ne - 1):
         back_home(d).start()
-    keep = pltpu.make_async_copy(done.at[own_rows, :], out.at[own_rows, :], loc_sem.at[0])
+    keep = pltpu.make_async_copy(done.at[own_rows, :], out.at[rows_of(mine), :], loc_sem.at[0])
     keep.start()
 
-    to_down.wait_send()
-    to_up.wait_send()
+    for n in range(8):
+        beside(n).wait_send()
 
     def drain_ring(t, carry):
         for c in range(2):
@@ -395,8 +415,9 @@
             pltpu.VMEM((cols // BS, 2, BS, BS), F32),
             pltpu.VMEM((2, 2 * half_rows, 256), F32),
             pltpu.VMEM((atoms + 8, 2 * W, BS), F32),
-            pltpu.VMEM((2, 4, 2 * W, BS), F32),
+            pltpu.VMEM((8, W, BS), F32),
             pltpu.VMEM((ne * 16, BS), F32),
+            pltpu.VMEM((ne, W, BS), F32),
             pltpu.VMEM((ne * 16, 3 * BS), F32),
             pltpu.VMEM((ne * 16, BS), F32),
             pltpu.VMEM((192, pairs), F32),
@@ -409,7 +430,7 @@
             dma((4,)),
             dma((4, LEVELS)), dma((4, LEVELS)),
             dma((4, LEVELS)), dma((4, LEVELS)),
-            dma((2,)), dma((2,)),
+            dma((8,)), dma((ne,)),
             dma((ne,)), dma((ne,)),
             dma((ne,)), dma((ne,)),
         ],

time: 64 us -> 61.8 us (0.966)
  Pallas kernels: 62.2 us -> 60 us
    pallas_call x1, Pallas kernels: 62.2 us -> 60 us  [per_device(): pl.pallas_call(functools.partial(main_kernel, ne), out_shape=jax.ShapeDty...]
where the time goes in v3:
time: 61.8 us; the launch traced here: 61.6 us
  Pallas kernels  60 us (97%)
  local copies, waits for them, and re-layouts  1.67 us (3%)
    pallas_call x1, Pallas kernels, per_device(): pl.pallas_call(functools.partial(main_kernel, ne), out_shape=jax.ShapeDty...  60 us
    unnamed x1, local copies, waits for them, and re-layouts  1.67 us

profile of v3, /device:TPU:1, one launch (start us, length us, event | category | flops | bytes accessed | tf_op | source)
XLA Modules:
  0.0 61.6 jit_solution(15173567720738855363)
XLA Ops:
  0.0 60.0 %lesser.1 = f32[512,128]{1,0:T(8,128)} custom-call(f32[2,256,2048]{2,1,0:T(8,128)} %bitcast.7, f32[2,2,128,128]{3,2,1,0:T(8,128)} %bitcast.10, f32[192,512]{1,0:T(8,128)} %bitcast.9, s32[16,32]{1,0:T(8,128)} %bitcast.11, s32[6]{0:T(128)} %shift.1, f32[2,6]{1,0:T(2,128)} %weight.1), custom_call_target="tpu_custom_call" | custom-call | tf_op jit(solution)/shard_map/lesser/pallas_call | solution.py:408
  60.0 1.7 %copy.8 = f32[1,512,128]{2,1,0:T(8,128)} copy(f32[1,512,128]{2,1,0:T(8,128)} %bitcast.8) | data formatting | bytes 524288

commit v4 on v3

--- a/solution.py
+++ b/solution.py
@@ -22,10 +22,6 @@
 BF16 = jnp.bfloat16
 
 
-def atom_of(e):
-    return e // 2 + 16 * (e % 2)
-
-
 def device_of(a):
     return 2 * (a % 16) + a // 16
 
@@ -49,7 +45,7 @@
 
 def main_kernel(
     ne, green, sigma, slab, nbt, shift, weight, out,
-    ext, sig, acc, bx, pair, rcv, rcv_n, half, done, slab_v, nbt_v, zed, zexp, bd, kmat, known,
+    ext, sig, acc, bx, pair, rcv, rcv_n, half, done, slab_v, nbt_v, zed, zexp, bd, bds, kmat, shift_s, weight_s, known,
     loc_sem, sig_send, sig_recv, halo_send, halo_recv, n_send, n_recv,
     a_send, a_recv, b_send, b_recv,
 ):
@@ -58,15 +54,21 @@
     up = lax.rem(me + 1, LEVELS)
     down = lax.rem(me + LEVELS - 1, LEVELS)
     rows = green.shape[1]
-    mine = atom_of(en)
     half_rows = rows // 2 + HALO
 
-    core, chip_x, chip_y = en % 2, en // 2 % SIDE, en // (2 * SIDE)
+    core, chip = lax.rem(en, 2), lax.div(en, 2)
+    chip_x, chip_y = lax.rem(chip, SIDE), lax.div(chip, SIDE)
+    at_y = [lax.rem(chip_y + n, SIDE) * SIDE for n in range(SIDE)]
+    at_x = [lax.rem(chip_x + n, SIDE) for n in range(SIDE)]
+    at_core = [core, 1 - core]
 
     def moved(dy, dx, dc):
-        return (
-            (chip_y + dy + SIDE) % SIDE * SIDE + (chip_x + dx + SIDE) % SIDE
-        ) * 2 + (core + dc) % 2
+        return (at_y[dy % SIDE] + at_x[dx % SIDE]) * 2 + at_core[dc % 2]
+
+    def atom_moved(dy, dx, dc):
+        return at_y[dy % SIDE] + at_x[dx % SIDE] + 16 * at_core[dc % 2]
+
+    mine = atom_moved(0, 0, 0)
 
     barrier = pltpu.get_barrier_semaphore()
     for z in (up, down):
@@ -87,6 +89,10 @@
     own_nbt = pltpu.make_async_copy(nbt, nbt_v, loc_sem.at[3])
     own_slab.start()
     own_nbt.start()
+    own_shift = pltpu.make_async_copy(shift, shift_s, loc_sem.at[4])
+    own_weight = pltpu.make_async_copy(weight, weight_s, loc_sem.at[5])
+    own_shift.start()
+    own_weight.start()
     own_sigma.start()
     own_green.start()
     pl.semaphore_wait(barrier, 7)
@@ -130,6 +136,8 @@
 
     own_slab.wait()
     own_nbt.wait()
+    own_shift.wait()
+    own_weight.wait()
     pairs = slab.shape[1]
     degree = nbt.shape[0]
     pick = (iota((pairs, BS), 0) == mine * degree + iota((pairs, BS), 1) // W).astype(F32)
@@ -151,12 +159,13 @@
             v = jnp.where(lane_l == i, zed[pl.ds(c * 64 + i * W, W), :], v)
         for d in range(2 * W):
             bd[pl.ds(d * W, W), pl.ds(c * BS, BS)] = jnp.where(place == float(d), v, 0.0)
+    bds[0], bds[1] = split(bd[...])
     delta = iota((ne, ne), 1) - iota((ne, ne), 0)
     k = jnp.zeros((ne, ne), F32)
     for q in range(shift.shape[0]):
-        k = k + jnp.where(delta == shift[q], weight[0, q], 0.0)
-        k = k + jnp.where(delta == -shift[q], weight[1, q], 0.0)
-    kmat[...] = k
+        k = k + jnp.where(delta == shift_s[q], weight_s[0, q], 0.0)
+        k = k + jnp.where(delta == -shift_s[q], weight_s[1, q], 0.0)
+    kmat[0], kmat[1] = split(k)
     acc[...] = jnp.zeros_like(acc)
 
     def widen(r, carry):
@@ -276,7 +285,7 @@
 
     def back(d):
         dy, dx, dc = FAR_FIRST[d]
-        return moved(-dy, -dx, dc)
+        return -dy, -dx, dc
 
     def rows_of(e):
         return pl.ds(pl.multiple_of(e * 16, 16), 16)
@@ -284,8 +293,8 @@
     def spread(d, source=None):
         to = there(d)
         return pltpu.make_async_remote_copy(
-            src_ref=bx.at[4 + atom_of(to)],
-            dst_ref=rcv.at[own_rows if source is None else rows_of(source), :],
+            src_ref=bx.at[4 + atom_moved(*FAR_FIRST[d])],
+            dst_ref=rcv.at[own_rows if source is None else rows_of(moved(*source)), :],
             send_sem=a_send.at[d], recv_sem=a_recv.at[d],
             device_id=(to, me), device_id_type=MESH,
         )
@@ -316,10 +325,10 @@
 
     xs = jnp.concatenate([rcv[pl.ds(r, ne, stride=16), :] for r in range(16)], axis=1)
     xh, xq = split(xs)
-    kh, kq = split(kmat[...])
+    kh, kq = kmat[0], kmat[1]
     ys = dot(kh, xh) + (dot(kh, xq) + dot(kq, xh))
     yh, yq = split(jnp.concatenate([ys[:, r * BS:(r + 1) * BS] for r in range(16)], axis=0))
-    bh, bq = split(bd[...])
+    bh, bq = bds[0], bds[1]
     half[...] = dot(yh, bh) + (dot(yh, bq) + dot(yq, bh))
 
     def conjugate(tile):
@@ -357,7 +366,7 @@
         to = there(d)
         return pltpu.make_async_remote_copy(
             src_ref=done.at[rows_of(to), :],
-            dst_ref=out.at[rows_of(mine if source is None else atom_of(source)), :],
+            dst_ref=out.at[rows_of(mine if source is None else atom_moved(*source)), :],
             send_sem=b_send.at[d], recv_sem=b_recv.at[d],
             device_id=(to, me), device_id_type=MESH,
         )
@@ -403,12 +412,11 @@
     half_rows = rows // 2 + HALO
     slab = dham.transpose(1, 2, 3, 0).reshape(192, pairs)
     anyspec = pl.BlockSpec(memory_space=pl.ANY)
-    smem = pl.BlockSpec(memory_space=pltpu.SMEM)
     dma = pltpu.SemaphoreType.DMA
     banded = pl.pallas_call(
         functools.partial(main_kernel, ne),
         out_shape=jax.ShapeDtypeStruct((pairs, BS), F32),
-        in_specs=[anyspec, anyspec, anyspec, anyspec, smem, smem],
+        in_specs=[anyspec] * 6,
         out_specs=anyspec,
         scratch_shapes=[
             pltpu.VMEM((2, rows + 2 * HALO, cols), F32),
@@ -425,9 +433,12 @@
             pltpu.VMEM((192, BS), F32),
             pltpu.VMEM((192, W, BS), F32),
             pltpu.VMEM((BS, 3 * BS), F32),
-            pltpu.VMEM((ne, ne), F32),
+            pltpu.VMEM((2, BS, 3 * BS), BF16),
+            pltpu.VMEM((2, ne, ne), BF16),
+            pltpu.SMEM((6,), jnp.int32),
+            pltpu.SMEM((2, 6), F32),
             pltpu.SemaphoreType.REGULAR((4,)),
-            dma((4,)),
+            dma((6,)),
             dma((4, LEVELS)), dma((4, LEVELS)),
             dma((4, LEVELS)), dma((4, LEVELS)),
             dma((8,)), dma((ne,)),
@@ -435,10 +446,13 @@
             dma((ne,)), dma((ne,)),
         ],
         compiler_params=pltpu.CompilerParams(
-            collective_id=0, has_side_effects=True, vmem_limit_bytes=64_000_000
+            collective_id=0, has_side_effects=True, vmem_limit_bytes=40_000_000
         ),
         name="lesser",
-    )(green[0], sigma[0], slab, neighbours.T, phonon_shift, phonon_weight)
+    )(*(
+        pltpu.with_memory_space_constraint(v, pltpu.HBM)
+        for v in (green[0], sigma[0], slab, neighbours.T, phonon_shift, phonon_weight)
+    ))
     return banded[None]
 
 

time: 61.8 us -> 59.9 us (0.969)
  local copies, waits for them, and re-layouts: 1.67 us -> 0.71 us
  Pallas kernels: 60 us -> 59.1 us
    unnamed x1, local copies, waits for them, and re-layouts: 1.67 us -> 0.71 us
    pallas_call x1, Pallas kernels: 60 us -> 59.1 us  [per_device(): pl.pallas_call(functools.partial(main_kernel, ne), out_shape=jax.ShapeDty...]
where the time goes in v4:
time: 59.9 us; the launch traced here: 59.8 us
  Pallas kernels  59.1 us (99%)
  local copies, waits for them, and re-layouts  0.71 us (1%)
    pallas_call x1, Pallas kernels, per_device(): pl.pallas_call(functools.partial(main_kernel, ne), out_shape=jax.ShapeDty...  59.1 us

profile of v4, /device:TPU:1, one launch (start us, length us, event | category | flops | bytes accessed | tf_op | source)
XLA Modules:
  0.0 59.8 jit_solution(9942393447316869064)
XLA Ops:
  0.0 59.1 %lesser.1 = f32[512,128]{1,0:T(8,128)S(1)} custom-call(f32[2,256,2048]{2,1,0:T(8,128)} %bitcast.8, f32[2,2,128,128]{3,2,1,0:T(8,128)} %bitcast.10, f32[192,512]{1,0:T(8,128)} %bitcast.9, s32[16,32]{1,0:T(8,128)} %bitcast.11, s32[6]{0:T(128)} %shift.1, f32[2,6]{1,0:T(2,128)} %weight.1), custom_call_target="tpu_custom_call" | custom-call | tf_op jit(solution)/shard_map/lesser/pallas_call | solution.py:416
  59.1 0.7 %copy.8 = f32[1,512,128]{2,1,0:T(8,128)} copy(f32[1,512,128]{2,1,0:T(8,128)S(1)} %bitcast.7) | data formatting | bytes 524288

commit v5 on v4

--- a/solution.py
+++ b/solution.py
@@ -274,8 +274,6 @@
         pair[n] = jnp.where(lane >= 96, re, im)
         re, im = bx[atoms + 4 + n, :W], pltpu.roll(bx[atoms + 4 + n, W:], 32, 1)
         pair[4 + n] = jnp.where(lane < 32, re, im)
-    for n in range(8):
-        beside(n).start()
     for i in range(16):
         extract(0, 4 + i)
         extract(1, i)
@@ -301,6 +299,8 @@
 
     for d in range(ne - 1):
         spread(d).start()
+    for n in range(8):
+        beside(n).start()
     rcv[own_rows, :] = bx[4 + mine]
 
     for d in range(ne - 1):

time: 59.9 us -> 59.9 us (level)
  no operation moved by 1% of the time
where the time goes in v5:
time: 59.9 us; the launch traced here: 59.8 us
  Pallas kernels  59.1 us (99%)
  local copies, waits for them, and re-layouts  0.71 us (1%)
    pallas_call x1, Pallas kernels, per_device(): pl.pallas_call(functools.partial(main_kernel, ne), out_shape=jax.ShapeDty...  59.1 us

profile of v5, /device:TPU:1, one launch (start us, length us, event | category | flops | bytes accessed | tf_op | source)
XLA Modules:
  0.0 59.8 jit_solution(9551489657609133569)
XLA Ops:
  0.0 59.1 %lesser.1 = f32[512,128]{1,0:T(8,128)S(1)} custom-call(f32[2,256,2048]{2,1,0:T(8,128)} %bitcast.8, f32[2,2,128,128]{3,2,1,0:T(8,128)} %bitcast.10, f32[192,512]{1,0:T(8,128)} %bitcast.9, s32[16,32]{1,0:T(8,128)} %bitcast.11, s32[6]{0:T(128)} %shift.1, f32[2,6]{1,0:T(2,128)} %weight.1), custom_call_target="tpu_custom_call" | custom-call | tf_op jit(solution)/shard_map/lesser/pallas_call | solution.py:416
  59.1 0.7 %copy.8 = f32[1,512,128]{2,1,0:T(8,128)} copy(f32[1,512,128]{2,1,0:T(8,128)S(1)} %bitcast.7) | data formatting | bytes 524288

commit v6 on v5

--- a/solution.py
+++ b/solution.py
@@ -336,7 +336,7 @@
         for z in range(2):
             t = [
                 half[
-                    pl.ds((z * W + j) * ne + tile * W, W),
+                    pl.ds(pl.multiple_of((z * W + j) * ne + tile * W, W), W),
                     pl.ds(c * BS, BS),
                 ]
                 for c in range(3) for j in range(W)
@@ -359,8 +359,8 @@
         for k in range(16):
             done[pl.ds(tile * BS + k, W, stride=16), :] = v[k]
 
-    for tile in range(ne // W):
-        conjugate(tile)
+    for off in (2, 1):
+        conjugate(lax.rem(chip_y + off, SIDE))
 
     def back_home(d, source=None):
         to = there(d)
@@ -372,7 +372,13 @@
         )
 
     for d in range(ne - 1):
-        back_home(d).start()
+        if FAR_FIRST[d][0] in (1, 2):
+            back_home(d).start()
+    for off in (3, 0):
+        conjugate(lax.rem(chip_y + off, SIDE))
+    for d in range(ne - 1):
+        if FAR_FIRST[d][0] not in (1, 2):
+            back_home(d).start()
     keep = pltpu.make_async_copy(done.at[own_rows, :], out.at[rows_of(mine), :], loc_sem.at[0])
     keep.start()
 

time: 59.9 us -> 59.8 us (level)
  no operation moved by 1% of the time
where the time goes in v6:
time: 59.8 us; the launch traced here: 59.7 us
  Pallas kernels  59 us (99%)
  local copies, waits for them, and re-layouts  0.71 us (1%)
    pallas_call x1, Pallas kernels, per_device(): pl.pallas_call(functools.partial(main_kernel, ne), out_shape=jax.ShapeDty...  59 us

profile of v6, /device:TPU:1, one launch (start us, length us, event | category | flops | bytes accessed | tf_op | source)
XLA Modules:
  0.0 59.7 jit_solution(8966527370714089642)
XLA Ops:
  0.0 59.0 %lesser.1 = f32[512,128]{1,0:T(8,128)S(1)} custom-call(f32[2,256,2048]{2,1,0:T(8,128)} %bitcast.8, f32[2,2,128,128]{3,2,1,0:T(8,128)} %bitcast.10, f32[192,512]{1,0:T(8,128)} %bitcast.9, s32[16,32]{1,0:T(8,128)} %bitcast.11, s32[6]{0:T(128)} %shift.1, f32[2,6]{1,0:T(2,128)} %weight.1), custom_call_target="tpu_custom_call" | custom-call | tf_op jit(solution)/shard_map/lesser/pallas_call | solution.py:422
  59.0 0.7 %copy.8 = f32[1,512,128]{2,1,0:T(8,128)} copy(f32[1,512,128]{2,1,0:T(8,128)S(1)} %bitcast.7) | data formatting | bytes 524288
